TPU v7x, 32 devices: a whole 2x2x4 slice. The times are simulated.
32 devices in a mesh: row: 4 (over y, x), col: 8 (over z, core).
Axes of the slice: x: 2, y: 2, z: 4, core: 2. Of those that a mesh axis runs over, the one named last changes fastest.
Arguments:
- coeffs: bfloat16 [16384, 2048], P('row'), may hold values from -1 to 1
- p_slots: int32 [4, 8, 64], P('row', 'col'), may hold values from 0 to 511, as said below
- p_count: int32 [4, 8], P('row', 'col'), may hold values from 1 to 64
- s_blocks: bfloat16 [4, 8, 64, 128, 128], P('row', 'col'), may hold values from -0.3984375 to 0.3984375
- s_slots: int32 [4, 8, 64], P('row', 'col'), may hold values from 0 to 511, as said below
- s_count: int32 [4, 8], P('row', 'col'), may hold values from 1 to 64
- q_slots: int32 [4, 8, 64], P('row', 'col'), may hold values from 0 to 511, as said below
- q_count: int32 [4, 8], P('row', 'col'), may hold values from 1 to 64
Outputs:
- density: bfloat16 [4, 8, 64, 128, 128], P('row', 'col')
- product: float32 [4, 8, 64, 128, 128], P('row', 'col')
Inputs may be any that keep to these rules, and one draw needn't show every extreme that they name: `p_slots`: on each device the live slots name different blocks of its tile; at least one device has all 64 slots live, which one is drawn. `s_slots`: on each device the live slots name different positions; at least one device has all 64 slots live, which one is drawn. `q_slots`: on each device the live slots name different blocks of its tile; at least one device has all 64 slots live, which one is drawn.
All inputs are finite; a program needn't handle non-finite values.
Results may differ from a plain program's by a relative error of at most 0.0029.
Values may be sent and summed in bfloat16 or wider, within the bound.
No kernel may reach another device: no remote copies, remote signals or barrier semaphores. Data moves between devices by JAX's collectives and lax.ppermute only.
A program may use at most 192 MiB of HBM per device.

v0:
```python
import jax
import jax.numpy as jnp
from jax import lax
from jax.sharding import PartitionSpec as P


def from_root(block, axis, source):
    block = jnp.where(lax.axis_index(axis) == source, block, jnp.zeros_like(block))
    return lax.psum(block, axis)


def shortened(shard):

    def short(part):
        return part.astype(jnp.bfloat16) if part.dtype == jnp.float32 else part

    return jax.tree.map(short, shard)


def shifted(block, axis, distance):
    devices = range(lax.axis_size(axis))
    route = [((i - distance) % len(devices), i) for i in devices]
    return lax.ppermute(block, axis, route)


def step_product(summed, p_data, s_data, panel_slot, q_row, q_col, tile_cols):
    p_blocks, p_code = p_data
    s_blocks, s_code = s_data
    local_k = jnp.arange(tile_cols, dtype=jnp.int32)
    p_live = p_code >= 0
    p_row = jnp.where(p_live, p_code // tile_cols, -1)
    p_col = jnp.where(p_live, p_code % tile_cols, -1)
    pick_left = (
        (p_row[:, None, None] == q_row[None, :, None])
        & (p_col[:, None, None] == local_k[None, None, :])
    ).astype(jnp.bfloat16)
    left_rows = jnp.einsum("pqk,pab->qakb", pick_left, p_blocks, preferred_element_type=jnp.float32)
    left_rows = left_rows.astype(jnp.bfloat16).reshape(q_row.shape[0], 128, tile_cols * 128)
    square = tile_cols * tile_cols
    s_live = (s_code >= 0) & (s_code // square == panel_slot)
    s_local = s_code % square
    s_row = jnp.where(s_live, s_local // tile_cols, -1)
    s_col = s_local % tile_cols
    pick_right = (
        (s_row[:, None, None] == local_k[None, :, None])
        & (s_col[:, None, None] == q_col[None, None, :])
    ).astype(jnp.bfloat16)
    right_cols = jnp.einsum(
        "skq,sab->kaqb", pick_right, s_blocks, preferred_element_type=jnp.float32
    )
    right_cols = right_cols.astype(jnp.bfloat16).reshape(tile_cols * 128, q_row.shape[0], 128)
    return summed + jnp.einsum(
        "qak,kqb->qab", left_rows, right_cols, preferred_element_type=jnp.float32
    )


def pick_tree(flag, moved, kept):
    return jax.tree.map(lambda fresh, stale: jnp.where(flag, fresh, stale), moved, kept)


def on_device(coeffs, p_slots, p_count, s_blocks, s_slots, s_count, q_slots, q_count):
    rows_n = lax.axis_size("row")
    cols_n = lax.axis_size("col")
    row_at = lax.axis_index("row")
    col_at = lax.axis_index("col")
    panel_rows, orbitals = coeffs.shape
    tile_rows = panel_rows // 128
    tile_cols = panel_rows * rows_n // cols_n // 128
    sub_span = cols_n // rows_n
    source = from_root(coeffs, "row", col_at // sub_span)
    column_rows = lax.dynamic_slice_in_dim(
        source, col_at % sub_span * (tile_cols * 128), tile_cols * 128, 0
    )
    slot_ids = p_slots[0, 0]
    p_max = slot_ids.shape[0]
    p_live = jnp.arange(p_max, dtype=jnp.int32) < p_count[0, 0]
    left = coeffs.reshape(tile_rows, 128, orbitals)[slot_ids // tile_cols]
    right = column_rows.reshape(tile_cols, 128, orbitals)[slot_ids % tile_cols]
    raw = jnp.einsum("pak,pbk->pab", left, right, preferred_element_type=jnp.float32)
    dense_blocks = jnp.where(p_live[:, None, None], raw, jnp.zeros_like(raw)).astype(jnp.bfloat16)
    p_code = jnp.where(p_live, slot_ids, -1)
    s_ids = s_slots[0, 0]
    s_max = s_ids.shape[0]
    s_live = jnp.arange(s_max, dtype=jnp.int32) < s_count[0, 0]
    s_code = jnp.where(s_live, s_ids, -1)
    s_local = s_blocks[0, 0]
    q_ids = q_slots[0, 0]
    q_max = q_ids.shape[0]
    q_live = jnp.arange(q_max, dtype=jnp.int32) < q_count[0, 0]
    q_row = q_ids // tile_cols
    q_col = q_ids % tile_cols
    zeros_out = jnp.zeros((q_max, 128, 128), jnp.float32)
    p_data = (dense_blocks, p_code)
    s_data = (s_local, s_code)
    level_count = rows_n.bit_length() - 1
    for level in range(level_count):
        moved = jax.tree.map(
            lambda part, own: part.astype(own.dtype),
            shifted(shortened(p_data), "col", -(1 << level)),
            p_data,
        )
        p_data = pick_tree(row_at >> level & 1 == 1, moved, p_data)
    row_offset = col_at % rows_n
    for level in range(level_count):
        moved = jax.tree.map(
            lambda part, own: part.astype(own.dtype),
            shifted(shortened(s_data), "row", -(1 << level)),
            s_data,
        )
        s_data = pick_tree(row_offset >> level & 1 == 1, moved, s_data)

    def advance(step_at, carry):
        summed, p_held, s_held = carry
        panel_at = (row_at + col_at + step_at) % cols_n
        summed = step_product(summed, p_held, s_held, panel_at // rows_n, q_row, q_col, tile_cols)
        p_held = jax.tree.map(
            lambda part, own: part.astype(own.dtype), shifted(shortened(p_held), "col", -1), p_held
        )
        s_held = jax.tree.map(
            lambda part, own: part.astype(own.dtype), shifted(shortened(s_held), "row", -1), s_held
        )
        return (summed, p_held, s_held)

    summed, p_data, s_data = lax.fori_loop(0, cols_n - 1, advance, (zeros_out, p_data, s_data))
    panel_at = (row_at + col_at + cols_n - 1) % cols_n
    summed = step_product(summed, p_data, s_data, panel_at // rows_n, q_row, q_col, tile_cols)
    product = jnp.where(q_live[:, None, None], summed, jnp.zeros_like(summed))
    return (dense_blocks.reshape(1, 1, p_max, 128, 128), product.reshape(1, 1, q_max, 128, 128))


def solution(mesh):
    return jax.shard_map(
        on_device,
        mesh=mesh,
        in_specs=(
            P("row", None),
            P("row", "col", None),
            P("row", "col"),
            P("row", "col", None, None, None),
            P("row", "col", None),
            P("row", "col"),
            P("row", "col", None),
            P("row", "col"),
        ),
        out_specs=(P("row", "col", None, None, None), P("row", "col", None, None, None)),
        check_vma=False,
    )
```

profile of v0, /device:TPU:0, one launch (start us, length us, event | category | flops | bytes accessed | tf_op | source)
XLA Modules:
  0.0 1880.5 jit_solution(13841358631608636264)
XLA Ops:
  7.2 13.8 broadcast_select_fusion
  26.0 19.3 %gather_fusion = bf16[64,128,2048]{2,1,0:T(8,128)(2,1)} fusion(bf16[32,128,2048]{2,1,0:T(8,128)(2,1)} %bitcast.130, s32[1024]{0:T(1024)S(1)} %get-tuple-element.386), kind=kCustom, calls=%fused_computation | custom fusion | bytes 67109120 | tf_op jit(solution)/shard_map/gather | solution.py:77
  45.3 329.8 %all-reduce.2.cloned.1.call-done = bf16[4096,2048]{1,0:T(8,128)(2,1)} async-done(((bf16[4096,2048]{1,0:T(8,128)(2,1)}), bf16[4096,2048]{1,0:T(8,128)(2,1)}) %all-reduce.2.cloned.1.call-update) | async-done | bytes 16777232 | tf_op jit(solution)/shard_map/psum | solution.py:9
  375.1 8.3 constant_dynamic-slice_fusion
  383.4 15.9 gather_fusion.1
  399.3 24.5 %select_convert_fusion = bf16[64,128,128]{2,1,0:T(8,128)(2,1)} fusion(pred[64]{0:T(512)(128)(4,1)S(1)} %iota_compare_fusion.5, bf16[64,128,2048]{2,1,0:T(8,128)(2,1)} %gather_fusion, bf16[64,128,2048]{2,1,0:T(8,128)(2,1)} %gather_fusion.1), kind=kOutput, calls=%fused_computation.45 | convolution fusion | flops 4297064448 | bytes 69206080 | tf_op jit(solution)/shard_map/pak,pbk->pab/dot_general | solution.py:79
  426.5 3.1 broadcast_select_fusion.1
  431.3 19.1 %collective-permute-done.4 = bf16[64,128,128]{2,1,0:T(8,128)(2,1)} collective-permute-done((bf16[64,128,128]{2,1,0:T(8,128)(2,1)}, bf16[64,128,128]{2,1,0:T(8,128)(2,1)}, u32[]{:S(2)}, u32[]{:S(2)}) %collective-permute-start.4) | collective-permute-done | bytes 2097184 | tf_op jit(solution)/shard_map/ppermute | solution.py:23
  450.4 3.1 broadcast_select_fusion.3
  462.1 35.9 %collective-permute-done.6 = s32[64]{0:T(128)S(1)} collective-permute-done((s32[64]{0:T(128)S(1)}, s32[64]{0:T(128)S(1)}, u32[]{:S(2)}, u32[]{:S(2)}) %collective-permute-start.6) | collective-permute-done | bytes 288 | tf_op jit(solution)/shard_map/ppermute | solution.py:23
  508.5 1178.6 %while.25 = (s32[]{:T(128)}, f32[64,128,128]{2,1,0:T(8,128)}, bf16[64,128,128]{2,0,1:T(8,128)(2,1)}, s32[64]{0:T(128)S(1)}, bf16[64,128,128]{2,0,1:T(8,128)(2,1)...) while((s32[]{:T(128)}, f32[64,128,128]{2,1,0:T(8,128)}, ...), condition=%wide.region_2.3_spmd.clone, body=%wide.region_1.2_spmd.clone.sunk | while | flops 8625731584 | bytes 239103024 | solution.py:124
  510.3 5.4 collective-permute-start
  522.3 13.8 convert_bitcast_fusion.4
  536.1 49.3 %reshape.448 = bf16[64,128,2048]{2,1,0:T(8,128)(2,1)} reshape(bf16[64,128,16,128]{3,2,1,0:T(8,128)(2,1)} %convert_bitcast_fusion.4) | data formatting | bytes 67108864 | tf_op jit(solution)/shard_map/while/body/eval_jaxpr/reshape | solution.py:38
  585.4 15.5 convolution_convert_fusion.2
  601.0 79.3 %select_add_fusion.2 = f32[64,128,128]{2,1,0:T(8,128)} fusion(f32[64,128,128]{2,1,0:T(8,128)} %get-tuple-element.471, pred[]{:T(512)S(6)} %compare.95, bf16[64,128,2048]{2,1,0:T(8,128)(2,1)} %reshape.448, bf16[2048,64,128]{2,1,0:T(8,128)(2,1)} %bitcast.128), kind=kOutput, calls=%fused_computation.6.clone.1 | convolution fusion | flops 4297064448 | bytes 75497472 | tf_op jit(solution)/shard_map/while/body/eval_jaxpr/qak,kqb->qab/dot_general | solution.py:52
  681.9 3.1 copy.48
  686.9 13.8 convert_bitcast_fusion.4
  700.7 49.3 %reshape.448 = bf16[64,128,2048]{2,1,0:T(8,128)(2,1)} reshape(bf16[64,128,16,128]{3,2,1,0:T(8,128)(2,1)} %convert_bitcast_fusion.4) | data formatting | bytes 67108864 | tf_op jit(solution)/shard_map/while/body/eval_jaxpr/reshape | solution.py:38
  750.0 15.5 convolution_convert_fusion.2
  765.6 80.5 %select_add_fusion.2 = f32[64,128,128]{2,1,0:T(8,128)} fusion(f32[64,128,128]{2,1,0:T(8,128)} %get-tuple-element.471, pred[]{:T(512)S(6)} %compare.95, bf16[64,128,2048]{2,1,0:T(8,128)(2,1)} %reshape.448, bf16[2048,64,128]{2,1,0:T(8,128)(2,1)} %bitcast.128), kind=kOutput, calls=%fused_computation.6.clone.1 | convolution fusion | flops 4297064448 | bytes 75497472 | tf_op jit(solution)/shard_map/while/body/eval_jaxpr/qak,kqb->qab/dot_general | solution.py:52
  855.7 13.8 convert_bitcast_fusion.4
  869.6 49.3 %reshape.448 = bf16[64,128,2048]{2,1,0:T(8,128)(2,1)} reshape(bf16[64,128,16,128]{3,2,1,0:T(8,128)(2,1)} %convert_bitcast_fusion.4) | data formatting | bytes 67108864 | tf_op jit(solution)/shard_map/while/body/eval_jaxpr/reshape | solution.py:38
  918.9 15.5 convolution_convert_fusion.2
  934.4 80.5 %select_add_fusion.2 = f32[64,128,128]{2,1,0:T(8,128)} fusion(f32[64,128,128]{2,1,0:T(8,128)} %get-tuple-element.471, pred[]{:T(512)S(6)} %compare.95, bf16[64,128,2048]{2,1,0:T(8,128)(2,1)} %reshape.448, bf16[2048,64,128]{2,1,0:T(8,128)(2,1)} %bitcast.128), kind=kOutput, calls=%fused_computation.6.clone.1 | convolution fusion | flops 4297064448 | bytes 75497472 | tf_op jit(solution)/shard_map/while/body/eval_jaxpr/qak,kqb->qab/dot_general | solution.py:52
  1021.8 13.8 convert_bitcast_fusion.4
  1035.7 49.3 %reshape.448 = bf16[64,128,2048]{2,1,0:T(8,128)(2,1)} reshape(bf16[64,128,16,128]{3,2,1,0:T(8,128)(2,1)} %convert_bitcast_fusion.4) | data formatting | bytes 67108864 | tf_op jit(solution)/shard_map/while/body/eval_jaxpr/reshape | solution.py:38
  1085.0 15.5 convolution_convert_fusion.2
  1100.5 80.5 %select_add_fusion.2 = f32[64,128,128]{2,1,0:T(8,128)} fusion(f32[64,128,128]{2,1,0:T(8,128)} %get-tuple-element.471, pred[]{:T(512)S(6)} %compare.95, bf16[64,128,2048]{2,1,0:T(8,128)(2,1)} %reshape.448, bf16[2048,64,128]{2,1,0:T(8,128)(2,1)} %bitcast.128), kind=kOutput, calls=%fused_computation.6.clone.1 | convolution fusion | flops 4297064448 | bytes 75497472 | tf_op jit(solution)/shard_map/while/body/eval_jaxpr/qak,kqb->qab/dot_general | solution.py:52
  1186.3 3.1 copy.48
  1192.9 13.8 convert_bitcast_fusion.4
  1206.8 49.3 %reshape.448 = bf16[64,128,2048]{2,1,0:T(8,128)(2,1)} reshape(bf16[64,128,16,128]{3,2,1,0:T(8,128)(2,1)} %convert_bitcast_fusion.4) | data formatting | bytes 67108864 | tf_op jit(solution)/shard_map/while/body/eval_jaxpr/reshape | solution.py:38
  1256.0 15.5 convolution_convert_fusion.2
  1271.6 80.5 %select_add_fusion.2 = f32[64,128,128]{2,1,0:T(8,128)} fusion(f32[64,128,128]{2,1,0:T(8,128)} %get-tuple-element.471, pred[]{:T(512)S(6)} %compare.95, bf16[64,128,2048]{2,1,0:T(8,128)(2,1)} %reshape.448, bf16[2048,64,128]{2,1,0:T(8,128)(2,1)} %bitcast.128), kind=kOutput, calls=%fused_computation.6.clone.1 | convolution fusion | flops 4297064448 | bytes 75497472 | tf_op jit(solution)/shard_map/while/body/eval_jaxpr/qak,kqb->qab/dot_general | solution.py:52
  1358.7 13.8 convert_bitcast_fusion.4
  1372.6 49.3 %reshape.448 = bf16[64,128,2048]{2,1,0:T(8,128)(2,1)} reshape(bf16[64,128,16,128]{3,2,1,0:T(8,128)(2,1)} %convert_bitcast_fusion.4) | data formatting | bytes 67108864 | tf_op jit(solution)/shard_map/while/body/eval_jaxpr/reshape | solution.py:38
  1421.9 15.5 convolution_convert_fusion.2
  1437.4 80.5 %select_add_fusion.2 = f32[64,128,128]{2,1,0:T(8,128)} fusion(f32[64,128,128]{2,1,0:T(8,128)} %get-tuple-element.471, pred[]{:T(512)S(6)} %compare.95, bf16[64,128,2048]{2,1,0:T(8,128)(2,1)} %reshape.448, bf16[2048,64,128]{2,1,0:T(8,128)(2,1)} %bitcast.128), kind=kOutput, calls=%fused_computation.6.clone.1 | convolution fusion | flops 4297064448 | bytes 75497472 | tf_op jit(solution)/shard_map/while/body/eval_jaxpr/qak,kqb->qab/dot_general | solution.py:52
  1527.6 13.8 convert_bitcast_fusion.4
  1541.4 49.3 %reshape.448 = bf16[64,128,2048]{2,1,0:T(8,128)(2,1)} reshape(bf16[64,128,16,128]{3,2,1,0:T(8,128)(2,1)} %convert_bitcast_fusion.4) | data formatting | bytes 67108864 | tf_op jit(solution)/shard_map/while/body/eval_jaxpr/reshape | solution.py:38
  1590.7 15.5 convolution_convert_fusion.2
  1606.2 80.5 %select_add_fusion.2 = f32[64,128,128]{2,1,0:T(8,128)} fusion(f32[64,128,128]{2,1,0:T(8,128)} %get-tuple-element.471, pred[]{:T(512)S(6)} %compare.95, bf16[64,128,2048]{2,1,0:T(8,128)(2,1)} %reshape.448, bf16[2048,64,128]{2,1,0:T(8,128)(2,1)} %bitcast.128), kind=kOutput, calls=%fused_computation.6.clone.1 | convolution fusion | flops 4297064448 | bytes 75497472 | tf_op jit(solution)/shard_map/while/body/eval_jaxpr/qak,kqb->qab/dot_general | solution.py:52
  1687.3 15.6 convert_bitcast_fusion.2
  1702.8 47.4 %copy.16 = bf16[64,128,16,128]{1,3,2,0:T(8,128)(2,1)} copy(bf16[64,128,16,128]{3,0,2,1:T(8,128)(2,1)} %convert_bitcast_fusion.2) | data formatting | bytes 67108864 | tf_op jit(solution)/shard_map/convert_element_type | solution.py:38
  1750.4 15.6 convert_bitcast_fusion.1
  1766.0 23.1 %copy.17 = bf16[16,128,64,128]{3,2,1,0:T(8,128)(2,1)} copy(bf16[16,128,64,128]{3,2,0,1:T(8,128)(2,1)} %convert_bitcast_fusion.1) | data formatting | bytes 67108864 | tf_op jit(solution)/shard_map/convert_element_type | solution.py:51
  1789.1 78.4 %fusion.14 = f32[64,128,128]{2,1,0:T(8,128)} fusion(bf16[64,128,2048]{1,2,0:T(8,128)(2,1)} %bitcast.131, bf16[2048,64,128]{2,1,0:T(8,128)(2,1)} %bitcast.132), kind=kOutput, calls=%fused_computation.39 | convolution fusion | flops 4294967296 | bytes 71303168 | tf_op jit(solution)/shard_map/qak,kqb->qab/dot_general | solution.py:52
  1867.5 5.9 select_bitcast_fusion
  (175 shorter events, 79.4 us)
Async XLA Ops:
  7.2 367.9 %all-reduce.2.cloned.1.call-start = ((), (), s32[]{:S(2)}) async-start(), calls=%async_computation | async-start | bytes 33554432 | tf_op jit(solution)/shard_map/psum | solution.py:9
  21.0 1.6 copy-start
  22.6 3.3 copy-start.2
  25.3 401.2 %collective-permute-start.8 = (bf16[64,128,128]{2,0,1:T(8,128)(2,1)}, bf16[64,128,128]{2,0,1:T(8,128)(2,1)}, u32[]{:S(2)}, u32[]{:S(2)}) collective-permute-start(bf16[64,128,128]{2,0,1:T(8,128)(2,1)} %bitcast.107), channel_id=1, source_target_pairs={{8,0},{16,8},{24,16},{0,24},{9,1},{17,9},{25,17},{1,25},{10,2},{18... | collective-permute-start | bytes 6291464 | tf_op jit(solution)/shard_map/ppermute | solution.py:23
  423.8 26.5 %collective-permute-start.4 = (bf16[64,128,128]{2,1,0:T(8,128)(2,1)}, bf16[64,128,128]{2,1,0:T(8,128)(2,1)}, u32[]{:S(2)}, u32[]{:S(2)}) collective-permute-start(bf16[64,128,128]{2,1,0:T(8,128)(2,1)} %select_convert_fusion), channel_id=1, source_target_pairs={{1,0},{2,1},{3,2},{4,3},{5,4},{6,5},{7,6},{0,7},{9,8},{10,9},{11,1... | collective-permute-start | bytes 6291464 | tf_op jit(solution)/shard_map/ppermute | solution.py:23
  429.6 28.3 %copy-start.3 = (s32[1,1,64]{2,1,0:T(1,128)S(1)}, s32[1,1,64]{2,1,0:T(1,128)}, u32[]{:S(2)}) copy-start(s32[1,1,64]{2,1,0:T(1,128)} %param.14) | copy-start | bytes 772
  429.6 31.9 %copy-start.5 = (s32[1,1,64]{2,1,0:T(1,128)S(1)}, s32[1,1,64]{2,1,0:T(1,128)}, u32[]{:S(2)}) copy-start(s32[1,1,64]{2,1,0:T(1,128)} %param.16) | copy-start | bytes 772
  429.7 72.8 %collective-permute-start.9 = (bf16[64,128,128]{2,0,1:T(8,128)(2,1)S(1)}, bf16[64,128,128]{2,0,1:T(8,128)(2,1)}, u32[]{:S(2)}, u32[]{:S(2)}) collective-permute-start(bf16[64,128,128]{2,0,1:T(8,128)(2,1)S(1)} %broadcast_select_fusion.1), channel_id=1, source_target_pairs={{16,0},{24,8},{0,16},{8,24},{17,1},{25,9},{1,17},{9,25},{18,2},{26... | collective-permute-start | bytes 6291464 | tf_op jit(solution)/shard_map/ppermute | solution.py:23
  453.5 50.5 %collective-permute-start.5 = (bf16[64,128,128]{2,1,0:T(8,128)(2,1)}, bf16[64,128,128]{2,1,0:T(8,128)(2,1)}, u32[]{:S(2)}, u32[]{:S(2)}) collective-permute-start(bf16[64,128,128]{2,1,0:T(8,128)(2,1)} %broadcast_select_fusion.3), channel_id=1, source_target_pairs={{2,0},{3,1},{4,2},{5,3},{6,4},{7,5},{0,6},{1,7},{10,8},{11,9},{12,... | collective-permute-start | bytes 6291464 | tf_op jit(solution)/shard_map/ppermute | solution.py:23
  454.2 43.9 %collective-permute-start.6 = (s32[64]{0:T(128)S(1)}, s32[64]{0:T(128)S(1)}, u32[]{:S(2)}, u32[]{:S(2)}) collective-permute-start(s32[64]{0:T(128)S(1)} %bitcast_select_fusion), channel_id=1, source_target_pairs={{1,0},{2,1},{3,2},{4,3},{5,4},{6,5},{7,6},{0,7},{9,8},{10,9},{11,1... | collective-permute-start | bytes 776 | tf_op jit(solution)/shard_map/ppermute | solution.py:23
  457.9 40.9 %collective-permute-start.10 = (s32[64]{0:T(128)S(1)}, s32[64]{0:T(128)S(1)}, u32[]{:S(2)}, u32[]{:S(2)}) collective-permute-start(s32[64]{0:T(128)S(1)} %compare_select_fusion.15), channel_id=1, source_target_pairs={{8,0},{16,8},{24,16},{0,24},{9,1},{17,9},{25,17},{1,25},{10,2},{18... | collective-permute-start | bytes 776 | tf_op jit(solution)/shard_map/ppermute | solution.py:23
  498.0 3.8 collective-permute-start.7
  498.9 3.6 collective-permute-start.11
  510.3 170.0 %collective-permute-start = (bf16[64,128,128]{2,0,1:T(8,128)(2,1)S(1)}, bf16[64,128,128]{2,0,1:T(8,128)(2,1)}, u32[]{:S(2)}, u32[]{:S(2)}) collective-permute-start(bf16[64,128,128]{2,0,1:T(8,128)(2,1)S(1)} %copy.46), channel_id=1, source_target_pairs={{1,0},{2,1},{3,2},{4,3},{5,4},{6,5},{7,6},{0,7},{9,8},{10,9},{11,1... | collective-permute-start | bytes 6291464 | tf_op jit(solution)/shard_map/while/body/eval_jaxpr/ppermute | solution.py:23
  515.6 164.6 %collective-permute-start.1 = (s32[64]{0:T(128)S(1)}, s32[64]{0:T(128)S(1)}, u32[]{:S(2)}, u32[]{:S(2)}) collective-permute-start(s32[64]{0:T(128)S(1)} %copy.47), channel_id=1, source_target_pairs={{1,0},{2,1},{3,2},{4,3},{5,4},{6,5},{7,6},{0,7},{9,8},{10,9},{11,1... | collective-permute-start | bytes 776 | tf_op jit(solution)/shard_map/while/body/eval_jaxpr/ppermute | solution.py:23
  518.8 161.5 %collective-permute-start.2 = (bf16[64,128,128]{2,0,1:T(8,128)(2,1)}, bf16[64,128,128]{2,0,1:T(8,128)(2,1)}, u32[]{:S(2)}, u32[]{:S(2)}) collective-permute-start(bf16[64,128,128]{2,0,1:T(8,128)(2,1)} %copy.48), channel_id=1, source_target_pairs={{8,0},{16,8},{24,16},{0,24},{9,1},{17,9},{25,17},{1,25},{10,2},{18... | collective-permute-start | bytes 6291464 | tf_op jit(solution)/shard_map/while/body/eval_jaxpr/ppermute | solution.py:23
  521.4 158.8 %collective-permute-start.3 = (s32[64]{0:T(128)S(1)}, s32[64]{0:T(128)S(1)}, u32[]{:S(2)}, u32[]{:S(2)}) collective-permute-start(s32[64]{0:T(128)S(1)} %copy.49), channel_id=1, source_target_pairs={{8,0},{16,8},{24,16},{0,24},{9,1},{17,9},{25,17},{1,25},{10,2},{18... | collective-permute-start | bytes 776 | tf_op jit(solution)/shard_map/while/body/eval_jaxpr/ppermute | solution.py:23
  681.9 164.2 %collective-permute-start = (bf16[64,128,128]{2,0,1:T(8,128)(2,1)S(1)}, bf16[64,128,128]{2,0,1:T(8,128)(2,1)}, u32[]{:S(2)}, u32[]{:S(2)}) collective-permute-start(bf16[64,128,128]{2,0,1:T(8,128)(2,1)S(1)} %copy.46), channel_id=1, source_target_pairs={{1,0},{2,1},{3,2},{4,3},{5,4},{6,5},{7,6},{0,7},{9,8},{10,9},{11,1... | collective-permute-start | bytes 6291464 | tf_op jit(solution)/shard_map/while/body/eval_jaxpr/ppermute | solution.py:23
  681.9 164.2 %collective-permute-start.1 = (s32[64]{0:T(128)S(1)}, s32[64]{0:T(128)S(1)}, u32[]{:S(2)}, u32[]{:S(2)}) collective-permute-start(s32[64]{0:T(128)S(1)} %copy.47), channel_id=1, source_target_pairs={{1,0},{2,1},{3,2},{4,3},{5,4},{6,5},{7,6},{0,7},{9,8},{10,9},{11,1... | collective-permute-start | bytes 776 | tf_op jit(solution)/shard_map/while/body/eval_jaxpr/ppermute | solution.py:23
  685.0 161.1 %collective-permute-start.2 = (bf16[64,128,128]{2,0,1:T(8,128)(2,1)}, bf16[64,128,128]{2,0,1:T(8,128)(2,1)}, u32[]{:S(2)}, u32[]{:S(2)}) collective-permute-start(bf16[64,128,128]{2,0,1:T(8,128)(2,1)} %copy.48), channel_id=1, source_target_pairs={{8,0},{16,8},{24,16},{0,24},{9,1},{17,9},{25,17},{1,25},{10,2},{18... | collective-permute-start | bytes 6291464 | tf_op jit(solution)/shard_map/while/body/eval_jaxpr/ppermute | solution.py:23
  686.2 159.9 %collective-permute-start.3 = (s32[64]{0:T(128)S(1)}, s32[64]{0:T(128)S(1)}, u32[]{:S(2)}, u32[]{:S(2)}) collective-permute-start(s32[64]{0:T(128)S(1)} %copy.49), channel_id=1, source_target_pairs={{8,0},{16,8},{24,16},{0,24},{9,1},{17,9},{25,17},{1,25},{10,2},{18... | collective-permute-start | bytes 776 | tf_op jit(solution)/shard_map/while/body/eval_jaxpr/ppermute | solution.py:23
  847.7 167.2 %collective-permute-start = (bf16[64,128,128]{2,0,1:T(8,128)(2,1)S(1)}, bf16[64,128,128]{2,0,1:T(8,128)(2,1)}, u32[]{:S(2)}, u32[]{:S(2)}) collective-permute-start(bf16[64,128,128]{2,0,1:T(8,128)(2,1)S(1)} %copy.46), channel_id=1, source_target_pairs={{1,0},{2,1},{3,2},{4,3},{5,4},{6,5},{7,6},{0,7},{9,8},{10,9},{11,1... | collective-permute-start | bytes 6291464 | tf_op jit(solution)/shard_map/while/body/eval_jaxpr/ppermute | solution.py:23
  848.1 166.8 %collective-permute-start.1 = (s32[64]{0:T(128)S(1)}, s32[64]{0:T(128)S(1)}, u32[]{:S(2)}, u32[]{:S(2)}) collective-permute-start(s32[64]{0:T(128)S(1)} %copy.47), channel_id=1, source_target_pairs={{1,0},{2,1},{3,2},{4,3},{5,4},{6,5},{7,6},{0,7},{9,8},{10,9},{11,1... | collective-permute-start | bytes 776 | tf_op jit(solution)/shard_map/while/body/eval_jaxpr/ppermute | solution.py:23
  852.4 162.5 %collective-permute-start.2 = (bf16[64,128,128]{2,0,1:T(8,128)(2,1)}, bf16[64,128,128]{2,0,1:T(8,128)(2,1)}, u32[]{:S(2)}, u32[]{:S(2)}) collective-permute-start(bf16[64,128,128]{2,0,1:T(8,128)(2,1)} %copy.48), channel_id=1, source_target_pairs={{8,0},{16,8},{24,16},{0,24},{9,1},{17,9},{25,17},{1,25},{10,2},{18... | collective-permute-start | bytes 6291464 | tf_op jit(solution)/shard_map/while/body/eval_jaxpr/ppermute | solution.py:23
  854.9 160.0 %collective-permute-start.3 = (s32[64]{0:T(128)S(1)}, s32[64]{0:T(128)S(1)}, u32[]{:S(2)}, u32[]{:S(2)}) collective-permute-start(s32[64]{0:T(128)S(1)} %copy.49), channel_id=1, source_target_pairs={{8,0},{16,8},{24,16},{0,24},{9,1},{17,9},{25,17},{1,25},{10,2},{18... | collective-permute-start | bytes 776 | tf_op jit(solution)/shard_map/while/body/eval_jaxpr/ppermute | solution.py:23
  1016.5 164.5 %collective-permute-start = (bf16[64,128,128]{2,0,1:T(8,128)(2,1)S(1)}, bf16[64,128,128]{2,0,1:T(8,128)(2,1)}, u32[]{:S(2)}, u32[]{:S(2)}) collective-permute-start(bf16[64,128,128]{2,0,1:T(8,128)(2,1)S(1)} %copy.46), channel_id=1, source_target_pairs={{1,0},{2,1},{3,2},{4,3},{5,4},{6,5},{7,6},{0,7},{9,8},{10,9},{11,1... | collective-permute-start | bytes 6291464 | tf_op jit(solution)/shard_map/while/body/eval_jaxpr/ppermute | solution.py:23
  1016.5 164.5 %collective-permute-start.1 = (s32[64]{0:T(128)S(1)}, s32[64]{0:T(128)S(1)}, u32[]{:S(2)}, u32[]{:S(2)}) collective-permute-start(s32[64]{0:T(128)S(1)} %copy.47), channel_id=1, source_target_pairs={{1,0},{2,1},{3,2},{4,3},{5,4},{6,5},{7,6},{0,7},{9,8},{10,9},{11,1... | collective-permute-start | bytes 776 | tf_op jit(solution)/shard_map/while/body/eval_jaxpr/ppermute | solution.py:23
  1019.9 161.1 %collective-permute-start.2 = (bf16[64,128,128]{2,0,1:T(8,128)(2,1)}, bf16[64,128,128]{2,0,1:T(8,128)(2,1)}, u32[]{:S(2)}, u32[]{:S(2)}) collective-permute-start(bf16[64,128,128]{2,0,1:T(8,128)(2,1)} %copy.48), channel_id=1, source_target_pairs={{8,0},{16,8},{24,16},{0,24},{9,1},{17,9},{25,17},{1,25},{10,2},{18... | collective-permute-start | bytes 6291464 | tf_op jit(solution)/shard_map/while/body/eval_jaxpr/ppermute | solution.py:23
  1021.1 159.9 %collective-permute-start.3 = (s32[64]{0:T(128)S(1)}, s32[64]{0:T(128)S(1)}, u32[]{:S(2)}, u32[]{:S(2)}) collective-permute-start(s32[64]{0:T(128)S(1)} %copy.49), channel_id=1, source_target_pairs={{8,0},{16,8},{24,16},{0,24},{9,1},{17,9},{25,17},{1,25},{10,2},{18... | collective-permute-start | bytes 776 | tf_op jit(solution)/shard_map/while/body/eval_jaxpr/ppermute | solution.py:23
  1182.6 169.5 %collective-permute-start = (bf16[64,128,128]{2,0,1:T(8,128)(2,1)S(1)}, bf16[64,128,128]{2,0,1:T(8,128)(2,1)}, u32[]{:S(2)}, u32[]{:S(2)}) collective-permute-start(bf16[64,128,128]{2,0,1:T(8,128)(2,1)S(1)} %copy.46), channel_id=1, source_target_pairs={{1,0},{2,1},{3,2},{4,3},{5,4},{6,5},{7,6},{0,7},{9,8},{10,9},{11,1... | collective-permute-start | bytes 6291464 | tf_op jit(solution)/shard_map/while/body/eval_jaxpr/ppermute | solution.py:23
  1184.0 168.1 %collective-permute-start.1 = (s32[64]{0:T(128)S(1)}, s32[64]{0:T(128)S(1)}, u32[]{:S(2)}, u32[]{:S(2)}) collective-permute-start(s32[64]{0:T(128)S(1)} %copy.47), channel_id=1, source_target_pairs={{1,0},{2,1},{3,2},{4,3},{5,4},{6,5},{7,6},{0,7},{9,8},{10,9},{11,1... | collective-permute-start | bytes 776 | tf_op jit(solution)/shard_map/while/body/eval_jaxpr/ppermute | solution.py:23
  1189.4 162.7 %collective-permute-start.2 = (bf16[64,128,128]{2,0,1:T(8,128)(2,1)}, bf16[64,128,128]{2,0,1:T(8,128)(2,1)}, u32[]{:S(2)}, u32[]{:S(2)}) collective-permute-start(bf16[64,128,128]{2,0,1:T(8,128)(2,1)} %copy.48), channel_id=1, source_target_pairs={{8,0},{16,8},{24,16},{0,24},{9,1},{17,9},{25,17},{1,25},{10,2},{18... | collective-permute-start | bytes 6291464 | tf_op jit(solution)/shard_map/while/body/eval_jaxpr/ppermute | solution.py:23
  1192.1 160.0 %collective-permute-start.3 = (s32[64]{0:T(128)S(1)}, s32[64]{0:T(128)S(1)}, u32[]{:S(2)}, u32[]{:S(2)}) collective-permute-start(s32[64]{0:T(128)S(1)} %copy.49), channel_id=1, source_target_pairs={{8,0},{16,8},{24,16},{0,24},{9,1},{17,9},{25,17},{1,25},{10,2},{18... | collective-permute-start | bytes 776 | tf_op jit(solution)/shard_map/while/body/eval_jaxpr/ppermute | solution.py:23
  1353.7 164.2 %collective-permute-start = (bf16[64,128,128]{2,0,1:T(8,128)(2,1)S(1)}, bf16[64,128,128]{2,0,1:T(8,128)(2,1)}, u32[]{:S(2)}, u32[]{:S(2)}) collective-permute-start(bf16[64,128,128]{2,0,1:T(8,128)(2,1)S(1)} %copy.46), channel_id=1, source_target_pairs={{1,0},{2,1},{3,2},{4,3},{5,4},{6,5},{7,6},{0,7},{9,8},{10,9},{11,1... | collective-permute-start | bytes 6291464 | tf_op jit(solution)/shard_map/while/body/eval_jaxpr/ppermute | solution.py:23
  1353.7 164.2 %collective-permute-start.1 = (s32[64]{0:T(128)S(1)}, s32[64]{0:T(128)S(1)}, u32[]{:S(2)}, u32[]{:S(2)}) collective-permute-start(s32[64]{0:T(128)S(1)} %copy.47), channel_id=1, source_target_pairs={{1,0},{2,1},{3,2},{4,3},{5,4},{6,5},{7,6},{0,7},{9,8},{10,9},{11,1... | collective-permute-start | bytes 776 | tf_op jit(solution)/shard_map/while/body/eval_jaxpr/ppermute | solution.py:23
  1356.8 161.1 %collective-permute-start.2 = (bf16[64,128,128]{2,0,1:T(8,128)(2,1)}, bf16[64,128,128]{2,0,1:T(8,128)(2,1)}, u32[]{:S(2)}, u32[]{:S(2)}) collective-permute-start(bf16[64,128,128]{2,0,1:T(8,128)(2,1)} %copy.48), channel_id=1, source_target_pairs={{8,0},{16,8},{24,16},{0,24},{9,1},{17,9},{25,17},{1,25},{10,2},{18... | collective-permute-start | bytes 6291464 | tf_op jit(solution)/shard_map/while/body/eval_jaxpr/ppermute | solution.py:23
  1358.0 159.9 %collective-permute-start.3 = (s32[64]{0:T(128)S(1)}, s32[64]{0:T(128)S(1)}, u32[]{:S(2)}, u32[]{:S(2)}) collective-permute-start(s32[64]{0:T(128)S(1)} %copy.49), channel_id=1, source_target_pairs={{8,0},{16,8},{24,16},{0,24},{9,1},{17,9},{25,17},{1,25},{10,2},{18... | collective-permute-start | bytes 776 | tf_op jit(solution)/shard_map/while/body/eval_jaxpr/ppermute | solution.py:23
  1519.5 167.2 %collective-permute-start = (bf16[64,128,128]{2,0,1:T(8,128)(2,1)S(1)}, bf16[64,128,128]{2,0,1:T(8,128)(2,1)}, u32[]{:S(2)}, u32[]{:S(2)}) collective-permute-start(bf16[64,128,128]{2,0,1:T(8,128)(2,1)S(1)} %copy.46), channel_id=1, source_target_pairs={{1,0},{2,1},{3,2},{4,3},{5,4},{6,5},{7,6},{0,7},{9,8},{10,9},{11,1... | collective-permute-start | bytes 6291464 | tf_op jit(solution)/shard_map/while/body/eval_jaxpr/ppermute | solution.py:23
  1519.5 167.2 %collective-permute-start.1 = (s32[64]{0:T(128)S(1)}, s32[64]{0:T(128)S(1)}, u32[]{:S(2)}, u32[]{:S(2)}) collective-permute-start(s32[64]{0:T(128)S(1)} %copy.47), channel_id=1, source_target_pairs={{1,0},{2,1},{3,2},{4,3},{5,4},{6,5},{7,6},{0,7},{9,8},{10,9},{11,1... | collective-permute-start | bytes 776 | tf_op jit(solution)/shard_map/while/body/eval_jaxpr/ppermute | solution.py:23
  1524.2 162.5 %collective-permute-start.2 = (bf16[64,128,128]{2,0,1:T(8,128)(2,1)}, bf16[64,128,128]{2,0,1:T(8,128)(2,1)}, u32[]{:S(2)}, u32[]{:S(2)}) collective-permute-start(bf16[64,128,128]{2,0,1:T(8,128)(2,1)} %copy.48), channel_id=1, source_target_pairs={{8,0},{16,8},{24,16},{0,24},{9,1},{17,9},{25,17},{1,25},{10,2},{18... | collective-permute-start | bytes 6291464 | tf_op jit(solution)/shard_map/while/body/eval_jaxpr/ppermute | solution.py:23
  1526.7 160.0 %collective-permute-start.3 = (s32[64]{0:T(128)S(1)}, s32[64]{0:T(128)S(1)}, u32[]{:S(2)}, u32[]{:S(2)}) collective-permute-start(s32[64]{0:T(128)S(1)} %copy.49), channel_id=1, source_target_pairs={{8,0},{16,8},{24,16},{0,24},{9,1},{17,9},{25,17},{1,25},{10,2},{18... | collective-permute-start | bytes 776 | tf_op jit(solution)/shard_map/while/body/eval_jaxpr/ppermute | solution.py:23
  1702.8 47.5 %copy-start.4 = (s32[64]{0:T(128)S(1)}, s32[64]{0:T(128)}, u32[]{:S(2)}) copy-start(s32[64]{0:T(128)} %fusion.26) | copy-start | bytes 772
  1789.1 78.4 %copy-start.1 = (pred[64]{0:T(512)(128)(4,1)S(1)}, pred[64]{0:T(512)(128)(4,1)}, u32[]{:S(2)}) copy-start(pred[64]{0:T(512)(128)(4,1)} %iota_compare_fusion.4) | copy-start | bytes 196
Sparse Core Ops, SparseCore 0:
  21.1 353.9 all-reduce.1
where the time goes:
time: 1900 us; the launch traced here: 1880 us
  matrix products  902 us (47%)
  local copies, waits for them, and re-layouts  499 us (26%)
  waiting for transfers between devices  387 us (20%)
  starting transfers between devices  43.5 us (2%)
  other arithmetic  31.6 us (2%)
    dot_general x8, matrix products, step_product(): jnp.einsum('qak,kqb->qab', left_rows, right_cols, preferred_element_type=...  641 us
    reshape x7, local copies, waits for them, and re-layouts, step_product(): left_rows.astype(jnp.bfloat16).reshape(q_row.shape[0], 128, tile_cols * 128)  345 us
    psum x1, waiting for transfers between devices, from_root(): return lax.psum(block, axis)  330 us
    dot_general x8, matrix products, step_product(): jnp.einsum('skq,sab->kaqb', pick_right, s_blocks, preferred_element_type=...  124 us
    dot_general x8, matrix products, step_product(): jnp.einsum('pqk,pab->qakb', pick_left, p_blocks, preferred_element_type=j...  112 us
    ppermute x36, waiting for transfers between devices, shifted(): return lax.ppermute(block, axis, route)  56.9 us
    convert_element_type x1, local copies, waits for them, and re-layouts, step_product(): left_rows.astype(jnp.bfloat16).reshape(q_row.shape[0], 128, tile_cols * 128)  47.4 us
    ppermute x36, starting transfers between devices, shifted(): return lax.ppermute(block, axis, route)  43.4 us
  transfers between devices with their start and end apart: 37, of which 5 were waited for; matrix products, arithmetic and copies ran while one was open for 65% of the time, Pallas kernels for 0%

commit v1 on v0

--- a/solution.py
+++ b/solution.py
@@ -6,7 +6,7 @@
 
 def from_root(block, axis, source):
     block = jnp.where(lax.axis_index(axis) == source, block, jnp.zeros_like(block))
-    return lax.psum(block, axis)
+    return jnp.sum(lax.all_gather(block, axis), axis=0)
 
 
 def shortened(shard):

time: 1900 us -> 2180 us (1.15)
  waiting for transfers between devices: 387 us -> 626 us
  other arithmetic: 31.6 us -> 62 us
    all_gather x0 -> x1, waiting for transfers between devices: none -> 568 us  [from_root(): return jnp.sum(lax.all_gather(block, axis), axis=0)]
    psum x1 -> x0, waiting for transfers between devices: 330 us -> none  [from_root(): return lax.psum(block, axis)]
    reduce_sum x0 -> x1, other arithmetic: none -> 30.4 us  [from_root(): return jnp.sum(lax.all_gather(block, axis), axis=0)]
  transfers between devices with their start and end apart: 37 -> 37, of which waited for: 5 -> 4; matrix products, arithmetic and copies ran while one was open for 65% -> 58% of each run, Pallas kernels for 0% -> 0%
where the time goes in v1:
time: 2180 us; the launch traced here: 2160 us
  matrix products  902 us (41%)
  waiting for transfers between devices  626 us (29%)
  local copies, waits for them, and re-layouts  510 us (23%)
  other arithmetic  62 us (3%)
  starting transfers between devices  40.1 us (2%)
    dot_general x8, matrix products, step_product(): jnp.einsum('qak,kqb->qab', left_rows, right_cols, preferred_element_type=...  641 us
    all_gather x1, waiting for transfers between devices, from_root(): return jnp.sum(lax.all_gather(block, axis), axis=0)  568 us
    reshape x7, local copies, waits for them, and re-layouts, step_product(): left_rows.astype(jnp.bfloat16).reshape(q_row.shape[0], 128, tile_cols * 128)  345 us
    dot_general x8, matrix products, step_product(): jnp.einsum('skq,sab->kaqb', pick_right, s_blocks, preferred_element_type=...  124 us
    dot_general x8, matrix products, step_product(): jnp.einsum('pqk,pab->qakb', pick_left, p_blocks, preferred_element_type=j...  113 us
    ppermute x36, waiting for transfers between devices, shifted(): return lax.ppermute(block, axis, route)  57.9 us
    convert_element_type x1, local copies, waits for them, and re-layouts, step_product(): left_rows.astype(jnp.bfloat16).reshape(q_row.shape[0], 128, tile_cols * 128)  47.5 us
  transfers between devices with their start and end apart: 37, of which 4 were waited for; matrix products, arithmetic and copies ran while one was open for 58% of the time, Pallas kernels for 0%

profile of v1, /device:TPU:0, one launch (start us, length us, event | category | flops | bytes accessed | tf_op | source)
XLA Modules:
  0.0 2157.2 jit_solution(15117901549779162671)
XLA Ops:
  7.2 13.8 broadcast_select_fusion
  26.0 30.1 %gather_fusion = bf16[64,128,2048]{2,1,0:T(8,128)(2,1)} fusion(bf16[32,128,2048]{2,1,0:T(8,128)(2,1)} %bitcast.131, s32[1024]{0:T(1024)S(1)} %get-tuple-element.386), kind=kCustom, calls=%fused_computation | custom fusion | bytes 67109120 | tf_op jit(solution)/shard_map/gather | solution.py:77
  56.1 567.7 %all-gather.3.cloned.1.call-done = bf16[16384,2048]{1,0:T(8,128)(2,1)} async-done(((bf16[4096,2048]{1,0:T(8,128)(2,1)}), bf16[16384,2048]{1,0:T(8,128)(2,1)}) %all-gather.3.cloned.1.call-update) | async-done | bytes 67108880 | tf_op jit(solution)/shard_map/all_gather | solution.py:9
  623.8 30.4 %reduce_sum.12 = bf16[4096,2048]{1,0:T(8,128)(2,1)} reduce(bf16[4,4096,2048]{2,1,0:T(8,128)(2,1)} %bitcast.4, bf16[]{:T(256)} %constant.359.clone.1), dimensions={0}, to_apply=%region_0.1 | reduce | flops 25165824 | bytes 83886080 | tf_op jit(solution)/shard_map/reduce_sum | solution.py:9
  654.2 8.3 constant_dynamic-slice_fusion
  662.5 15.8 gather_fusion.1
  678.3 24.5 %select_convert_fusion = bf16[64,128,128]{2,1,0:T(8,128)(2,1)} fusion(pred[64]{0:T(512)(128)(4,1)S(1)} %iota_compare_fusion.5, bf16[64,128,2048]{2,1,0:T(8,128)(2,1)} %gather_fusion, bf16[64,128,2048]{2,1,0:T(8,128)(2,1)} %gather_fusion.1), kind=kOutput, calls=%fused_computation.45 | convolution fusion | flops 4297064448 | bytes 69206080 | tf_op jit(solution)/shard_map/pak,pbk->pab/dot_general | solution.py:79
  706.5 3.1 broadcast_select_fusion.1
  711.2 18.5 collective-permute-done.4
  729.7 3.1 broadcast_select_fusion.3
  741.1 36.3 %collective-permute-done.6 = s32[64]{0:T(128)S(1)} collective-permute-done((s32[64]{0:T(128)S(1)}, s32[64]{0:T(128)S(1)}, u32[]{:S(2)}, u32[]{:S(2)}) %collective-permute-start.6) | collective-permute-done | bytes 288 | tf_op jit(solution)/shard_map/ppermute | solution.py:23
  787.2 1176.3 %while.25 = (s32[]{:T(128)}, f32[64,128,128]{2,1,0:T(8,128)}, bf16[64,128,128]{2,0,1:T(8,128)(2,1)}, s32[64]{0:T(128)S(1)}, bf16[64,128,128]{2,0,1:T(8,128)(2,1)...) while((s32[]{:T(128)}, f32[64,128,128]{2,1,0:T(8,128)}, ...), condition=%wide.region_2.3_spmd.clone, body=%wide.region_1.2_spmd.clone.sunk | while | flops 8625731584 | bytes 239103024 | solution.py:124
  789.0 6.0 collective-permute-start
  801.4 13.9 convert_bitcast_fusion.4
  815.2 49.3 %reshape.449 = bf16[64,128,2048]{2,1,0:T(8,128)(2,1)} reshape(bf16[64,128,16,128]{3,2,1,0:T(8,128)(2,1)} %convert_bitcast_fusion.4) | data formatting | bytes 67108864 | tf_op jit(solution)/shard_map/while/body/eval_jaxpr/reshape | solution.py:38
  864.5 15.5 convolution_convert_fusion.2
  880.0 79.3 %select_add_fusion.2 = f32[64,128,128]{2,1,0:T(8,128)} fusion(f32[64,128,128]{2,1,0:T(8,128)} %get-tuple-element.471, pred[]{:T(512)S(6)} %compare.95, bf16[64,128,2048]{2,1,0:T(8,128)(2,1)} %reshape.449, bf16[2048,64,128]{2,1,0:T(8,128)(2,1)} %bitcast.129), kind=kOutput, calls=%fused_computation.6.clone.1 | convolution fusion | flops 4297064448 | bytes 75497472 | tf_op jit(solution)/shard_map/while/body/eval_jaxpr/qak,kqb->qab/dot_general | solution.py:52
  966.1 13.8 convert_bitcast_fusion.4
  980.0 49.3 %reshape.449 = bf16[64,128,2048]{2,1,0:T(8,128)(2,1)} reshape(bf16[64,128,16,128]{3,2,1,0:T(8,128)(2,1)} %convert_bitcast_fusion.4) | data formatting | bytes 67108864 | tf_op jit(solution)/shard_map/while/body/eval_jaxpr/reshape | solution.py:38
  1029.3 15.5 convolution_convert_fusion.2
  1044.8 80.5 %select_add_fusion.2 = f32[64,128,128]{2,1,0:T(8,128)} fusion(f32[64,128,128]{2,1,0:T(8,128)} %get-tuple-element.471, pred[]{:T(512)S(6)} %compare.95, bf16[64,128,2048]{2,1,0:T(8,128)(2,1)} %reshape.449, bf16[2048,64,128]{2,1,0:T(8,128)(2,1)} %bitcast.129), kind=kOutput, calls=%fused_computation.6.clone.1 | convolution fusion | flops 4297064448 | bytes 75497472 | tf_op jit(solution)/shard_map/while/body/eval_jaxpr/qak,kqb->qab/dot_general | solution.py:52
  1133.3 13.8 convert_bitcast_fusion.4
  1147.2 49.3 %reshape.449 = bf16[64,128,2048]{2,1,0:T(8,128)(2,1)} reshape(bf16[64,128,16,128]{3,2,1,0:T(8,128)(2,1)} %convert_bitcast_fusion.4) | data formatting | bytes 67108864 | tf_op jit(solution)/shard_map/while/body/eval_jaxpr/reshape | solution.py:38
  1196.5 15.5 convolution_convert_fusion.2
  1212.0 80.5 %select_add_fusion.2 = f32[64,128,128]{2,1,0:T(8,128)} fusion(f32[64,128,128]{2,1,0:T(8,128)} %get-tuple-element.471, pred[]{:T(512)S(6)} %compare.95, bf16[64,128,2048]{2,1,0:T(8,128)(2,1)} %reshape.449, bf16[2048,64,128]{2,1,0:T(8,128)(2,1)} %bitcast.129), kind=kOutput, calls=%fused_computation.6.clone.1 | convolution fusion | flops 4297064448 | bytes 75497472 | tf_op jit(solution)/shard_map/while/body/eval_jaxpr/qak,kqb->qab/dot_general | solution.py:52
  1299.4 13.8 convert_bitcast_fusion.4
  1313.2 49.3 %reshape.449 = bf16[64,128,2048]{2,1,0:T(8,128)(2,1)} reshape(bf16[64,128,16,128]{3,2,1,0:T(8,128)(2,1)} %convert_bitcast_fusion.4) | data formatting | bytes 67108864 | tf_op jit(solution)/shard_map/while/body/eval_jaxpr/reshape | solution.py:38
  1362.5 15.5 convolution_convert_fusion.2
  1378.1 80.5 %select_add_fusion.2 = f32[64,128,128]{2,1,0:T(8,128)} fusion(f32[64,128,128]{2,1,0:T(8,128)} %get-tuple-element.471, pred[]{:T(512)S(6)} %compare.95, bf16[64,128,2048]{2,1,0:T(8,128)(2,1)} %reshape.449, bf16[2048,64,128]{2,1,0:T(8,128)(2,1)} %bitcast.129), kind=kOutput, calls=%fused_computation.6.clone.1 | convolution fusion | flops 4297064448 | bytes 75497472 | tf_op jit(solution)/shard_map/while/body/eval_jaxpr/qak,kqb->qab/dot_general | solution.py:52
  1460.2 4.2 collective-permute-start
  1470.8 13.8 convert_bitcast_fusion.4
  1484.6 49.3 %reshape.449 = bf16[64,128,2048]{2,1,0:T(8,128)(2,1)} reshape(bf16[64,128,16,128]{3,2,1,0:T(8,128)(2,1)} %convert_bitcast_fusion.4) | data formatting | bytes 67108864 | tf_op jit(solution)/shard_map/while/body/eval_jaxpr/reshape | solution.py:38
  1533.9 15.5 convolution_convert_fusion.2
  1549.5 80.5 %select_add_fusion.2 = f32[64,128,128]{2,1,0:T(8,128)} fusion(f32[64,128,128]{2,1,0:T(8,128)} %get-tuple-element.471, pred[]{:T(512)S(6)} %compare.95, bf16[64,128,2048]{2,1,0:T(8,128)(2,1)} %reshape.449, bf16[2048,64,128]{2,1,0:T(8,128)(2,1)} %bitcast.129), kind=kOutput, calls=%fused_computation.6.clone.1 | convolution fusion | flops 4297064448 | bytes 75497472 | tf_op jit(solution)/shard_map/while/body/eval_jaxpr/qak,kqb->qab/dot_general | solution.py:52
  1636.8 13.8 convert_bitcast_fusion.4
  1650.6 49.3 %reshape.449 = bf16[64,128,2048]{2,1,0:T(8,128)(2,1)} reshape(bf16[64,128,16,128]{3,2,1,0:T(8,128)(2,1)} %convert_bitcast_fusion.4) | data formatting | bytes 67108864 | tf_op jit(solution)/shard_map/while/body/eval_jaxpr/reshape | solution.py:38
  1699.9 15.5 convolution_convert_fusion.2
  1715.5 80.5 %select_add_fusion.2 = f32[64,128,128]{2,1,0:T(8,128)} fusion(f32[64,128,128]{2,1,0:T(8,128)} %get-tuple-element.471, pred[]{:T(512)S(6)} %compare.95, bf16[64,128,2048]{2,1,0:T(8,128)(2,1)} %reshape.449, bf16[2048,64,128]{2,1,0:T(8,128)(2,1)} %bitcast.129), kind=kOutput, calls=%fused_computation.6.clone.1 | convolution fusion | flops 4297064448 | bytes 75497472 | tf_op jit(solution)/shard_map/while/body/eval_jaxpr/qak,kqb->qab/dot_general | solution.py:52
  1804.0 13.8 convert_bitcast_fusion.4
  1817.8 49.3 %reshape.449 = bf16[64,128,2048]{2,1,0:T(8,128)(2,1)} reshape(bf16[64,128,16,128]{3,2,1,0:T(8,128)(2,1)} %convert_bitcast_fusion.4) | data formatting | bytes 67108864 | tf_op jit(solution)/shard_map/while/body/eval_jaxpr/reshape | solution.py:38
  1867.1 15.5 convolution_convert_fusion.2
  1882.6 80.5 %select_add_fusion.2 = f32[64,128,128]{2,1,0:T(8,128)} fusion(f32[64,128,128]{2,1,0:T(8,128)} %get-tuple-element.471, pred[]{:T(512)S(6)} %compare.95, bf16[64,128,2048]{2,1,0:T(8,128)(2,1)} %reshape.449, bf16[2048,64,128]{2,1,0:T(8,128)(2,1)} %bitcast.129), kind=kOutput, calls=%fused_computation.6.clone.1 | convolution fusion | flops 4297064448 | bytes 75497472 | tf_op jit(solution)/shard_map/while/body/eval_jaxpr/qak,kqb->qab/dot_general | solution.py:52
  1963.7 15.6 convert_bitcast_fusion.1
  1979.3 23.4 %copy.17 = bf16[16,128,64,128]{3,2,1,0:T(8,128)(2,1)} copy(bf16[16,128,64,128]{3,2,0,1:T(8,128)(2,1)} %convert_bitcast_fusion.1) | data formatting | bytes 67108864 | tf_op jit(solution)/shard_map/convert_element_type | solution.py:51
  2002.7 15.6 convert_bitcast_fusion.2
  2018.3 47.5 %copy.16 = bf16[64,128,16,128]{1,3,2,0:T(8,128)(2,1)} copy(bf16[64,128,16,128]{3,0,2,1:T(8,128)(2,1)} %convert_bitcast_fusion.2) | data formatting | bytes 67108864 | tf_op jit(solution)/shard_map/convert_element_type | solution.py:38
  2065.8 78.4 %fusion.14 = f32[64,128,128]{2,1,0:T(8,128)} fusion(bf16[64,128,2048]{1,2,0:T(8,128)(2,1)} %bitcast.133, bf16[2048,64,128]{2,1,0:T(8,128)(2,1)} %bitcast.132), kind=kOutput, calls=%fused_computation.39 | convolution fusion | flops 4294967296 | bytes 71303168 | tf_op jit(solution)/shard_map/qak,kqb->qab/dot_general | solution.py:52
  2144.2 5.9 select_bitcast_fusion
  (176 shorter events, 78.5 us)
Async XLA Ops:
  7.2 616.6 %all-gather.3.cloned.1.call-start = ((), (), s32[]{:S(2)}) async-start(), calls=%async_computation | async-start | bytes 83886080 | tf_op jit(solution)/shard_map/all_gather | solution.py:9
  21.0 1.6 copy-start
  22.6 3.3 copy-start.3
  25.3 681.2 %collective-permute-start.8 = (bf16[64,128,128]{2,0,1:T(8,128)(2,1)}, bf16[64,128,128]{2,0,1:T(8,128)(2,1)}, u32[]{:S(2)}, u32[]{:S(2)}) collective-permute-start(bf16[64,128,128]{2,0,1:T(8,128)(2,1)} %bitcast.108), channel_id=1, source_target_pairs={{8,0},{16,8},{24,16},{0,24},{9,1},{17,9},{25,17},{1,25},{10,2},{18... | collective-permute-start | bytes 6291464 | tf_op jit(solution)/shard_map/ppermute | solution.py:23
  702.8 26.9 %collective-permute-start.4 = (bf16[64,128,128]{2,1,0:T(8,128)(2,1)}, bf16[64,128,128]{2,1,0:T(8,128)(2,1)}, u32[]{:S(2)}, u32[]{:S(2)}) collective-permute-start(bf16[64,128,128]{2,1,0:T(8,128)(2,1)} %select_convert_fusion), channel_id=1, source_target_pairs={{1,0},{2,1},{3,2},{4,3},{5,4},{6,5},{7,6},{0,7},{9,8},{10,9},{11,1... | collective-permute-start | bytes 6291464 | tf_op jit(solution)/shard_map/ppermute | solution.py:23
  709.7 23.9 %copy-start.2 = (s32[1,1,64]{2,1,0:T(1,128)S(1)}, s32[1,1,64]{2,1,0:T(1,128)}, u32[]{:S(2)}) copy-start(s32[1,1,64]{2,1,0:T(1,128)} %param.14) | copy-start | bytes 772
  709.7 29.3 %copy-start.5 = (s32[1,1,64]{2,1,0:T(1,128)S(1)}, s32[1,1,64]{2,1,0:T(1,128)}, u32[]{:S(2)}) copy-start(s32[1,1,64]{2,1,0:T(1,128)} %param.16) | copy-start | bytes 772
  709.7 71.6 %collective-permute-start.9 = (bf16[64,128,128]{2,0,1:T(8,128)(2,1)S(1)}, bf16[64,128,128]{2,0,1:T(8,128)(2,1)}, u32[]{:S(2)}, u32[]{:S(2)}) collective-permute-start(bf16[64,128,128]{2,0,1:T(8,128)(2,1)S(1)} %broadcast_select_fusion.1), channel_id=1, source_target_pairs={{16,0},{24,8},{0,16},{8,24},{17,1},{25,9},{1,17},{9,25},{18,2},{26... | collective-permute-start | bytes 6291464 | tf_op jit(solution)/shard_map/ppermute | solution.py:23
  732.9 49.9 %collective-permute-start.5 = (bf16[64,128,128]{2,1,0:T(8,128)(2,1)}, bf16[64,128,128]{2,1,0:T(8,128)(2,1)}, u32[]{:S(2)}, u32[]{:S(2)}) collective-permute-start(bf16[64,128,128]{2,1,0:T(8,128)(2,1)} %broadcast_select_fusion.3), channel_id=1, source_target_pairs={{2,0},{3,1},{4,2},{5,3},{6,4},{7,5},{0,6},{1,7},{10,8},{11,9},{12,... | collective-permute-start | bytes 6291464 | tf_op jit(solution)/shard_map/ppermute | solution.py:23
  733.5 6.0 collective-permute-start.10
  735.0 42.4 %collective-permute-start.6 = (s32[64]{0:T(128)S(1)}, s32[64]{0:T(128)S(1)}, u32[]{:S(2)}, u32[]{:S(2)}) collective-permute-start(s32[64]{0:T(128)S(1)} %bitcast_select_fusion), channel_id=1, source_target_pairs={{1,0},{2,1},{3,2},{4,3},{5,4},{6,5},{7,6},{0,7},{9,8},{10,9},{11,1... | collective-permute-start | bytes 776 | tf_op jit(solution)/shard_map/ppermute | solution.py:23
  739.6 38.7 %collective-permute-start.11 = (s32[64]{0:T(128)S(1)}, s32[64]{0:T(128)S(1)}, u32[]{:S(2)}, u32[]{:S(2)}) collective-permute-start(s32[64]{0:T(128)S(1)} %broadcast_select_fusion.5), channel_id=1, source_target_pairs={{16,0},{24,8},{0,16},{8,24},{17,1},{25,9},{1,17},{9,25},{18,2},{26... | collective-permute-start | bytes 776 | tf_op jit(solution)/shard_map/ppermute | solution.py:23
  777.4 3.8 collective-permute-start.7
  787.2 1176.4 %copy-start.4 = (s32[64]{0:T(128)S(1)}, s32[64]{0:T(128)}, u32[]{:S(2)}) copy-start(s32[64]{0:T(128)} %fusion.26) | copy-start | bytes 772
  789.0 170.3 %collective-permute-start = (bf16[64,128,128]{2,0,1:T(8,128)(2,1)S(1)}, bf16[64,128,128]{2,0,1:T(8,128)(2,1)}, u32[]{:S(2)}, u32[]{:S(2)}) collective-permute-start(bf16[64,128,128]{2,0,1:T(8,128)(2,1)S(1)} %copy.45), channel_id=1, source_target_pairs={{1,0},{2,1},{3,2},{4,3},{5,4},{6,5},{7,6},{0,7},{9,8},{10,9},{11,1... | collective-permute-start | bytes 6291464 | tf_op jit(solution)/shard_map/while/body/eval_jaxpr/ppermute | solution.py:23
  798.1 161.2 %collective-permute-start.2 = (bf16[64,128,128]{2,0,1:T(8,128)(2,1)}, bf16[64,128,128]{2,0,1:T(8,128)(2,1)}, u32[]{:S(2)}, u32[]{:S(2)}) collective-permute-start(bf16[64,128,128]{2,0,1:T(8,128)(2,1)} %copy.47), channel_id=1, source_target_pairs={{8,0},{16,8},{24,16},{0,24},{9,1},{17,9},{25,17},{1,25},{10,2},{18... | collective-permute-start | bytes 6291464 | tf_op jit(solution)/shard_map/while/body/eval_jaxpr/ppermute | solution.py:23
  799.6 159.7 %collective-permute-start.1 = (s32[64]{0:T(128)S(1)}, s32[64]{0:T(128)S(1)}, u32[]{:S(2)}, u32[]{:S(2)}) collective-permute-start(s32[64]{0:T(128)S(1)} %copy.46), channel_id=1, source_target_pairs={{1,0},{2,1},{3,2},{4,3},{5,4},{6,5},{7,6},{0,7},{9,8},{10,9},{11,1... | collective-permute-start | bytes 776 | tf_op jit(solution)/shard_map/while/body/eval_jaxpr/ppermute | solution.py:23
  799.6 159.7 %collective-permute-start.3 = (s32[64]{0:T(128)S(1)}, s32[64]{0:T(128)S(1)}, u32[]{:S(2)}, u32[]{:S(2)}) collective-permute-start(s32[64]{0:T(128)S(1)} %copy.48), channel_id=1, source_target_pairs={{8,0},{16,8},{24,16},{0,24},{9,1},{17,9},{25,17},{1,25},{10,2},{18... | collective-permute-start | bytes 776 | tf_op jit(solution)/shard_map/while/body/eval_jaxpr/ppermute | solution.py:23
  961.0 164.4 %collective-permute-start = (bf16[64,128,128]{2,0,1:T(8,128)(2,1)S(1)}, bf16[64,128,128]{2,0,1:T(8,128)(2,1)}, u32[]{:S(2)}, u32[]{:S(2)}) collective-permute-start(bf16[64,128,128]{2,0,1:T(8,128)(2,1)S(1)} %copy.45), channel_id=1, source_target_pairs={{1,0},{2,1},{3,2},{4,3},{5,4},{6,5},{7,6},{0,7},{9,8},{10,9},{11,1... | collective-permute-start | bytes 6291464 | tf_op jit(solution)/shard_map/while/body/eval_jaxpr/ppermute | solution.py:23
  964.1 161.3 %collective-permute-start.2 = (bf16[64,128,128]{2,0,1:T(8,128)(2,1)}, bf16[64,128,128]{2,0,1:T(8,128)(2,1)}, u32[]{:S(2)}, u32[]{:S(2)}) collective-permute-start(bf16[64,128,128]{2,0,1:T(8,128)(2,1)} %copy.47), channel_id=1, source_target_pairs={{8,0},{16,8},{24,16},{0,24},{9,1},{17,9},{25,17},{1,25},{10,2},{18... | collective-permute-start | bytes 6291464 | tf_op jit(solution)/shard_map/while/body/eval_jaxpr/ppermute | solution.py:23
  965.5 159.8 %collective-permute-start.1 = (s32[64]{0:T(128)S(1)}, s32[64]{0:T(128)S(1)}, u32[]{:S(2)}, u32[]{:S(2)}) collective-permute-start(s32[64]{0:T(128)S(1)} %copy.46), channel_id=1, source_target_pairs={{1,0},{2,1},{3,2},{4,3},{5,4},{6,5},{7,6},{0,7},{9,8},{10,9},{11,1... | collective-permute-start | bytes 776 | tf_op jit(solution)/shard_map/while/body/eval_jaxpr/ppermute | solution.py:23
  965.5 159.8 %collective-permute-start.3 = (s32[64]{0:T(128)S(1)}, s32[64]{0:T(128)S(1)}, u32[]{:S(2)}, u32[]{:S(2)}) collective-permute-start(s32[64]{0:T(128)S(1)} %copy.48), channel_id=1, source_target_pairs={{8,0},{16,8},{24,16},{0,24},{9,1},{17,9},{25,17},{1,25},{10,2},{18... | collective-permute-start | bytes 776 | tf_op jit(solution)/shard_map/while/body/eval_jaxpr/ppermute | solution.py:23
  1126.9 165.6 %collective-permute-start = (bf16[64,128,128]{2,0,1:T(8,128)(2,1)S(1)}, bf16[64,128,128]{2,0,1:T(8,128)(2,1)}, u32[]{:S(2)}, u32[]{:S(2)}) collective-permute-start(bf16[64,128,128]{2,0,1:T(8,128)(2,1)S(1)} %copy.45), channel_id=1, source_target_pairs={{1,0},{2,1},{3,2},{4,3},{5,4},{6,5},{7,6},{0,7},{9,8},{10,9},{11,1... | collective-permute-start | bytes 6291464 | tf_op jit(solution)/shard_map/while/body/eval_jaxpr/ppermute | solution.py:23
  1130.1 162.4 %collective-permute-start.2 = (bf16[64,128,128]{2,0,1:T(8,128)(2,1)}, bf16[64,128,128]{2,0,1:T(8,128)(2,1)}, u32[]{:S(2)}, u32[]{:S(2)}) collective-permute-start(bf16[64,128,128]{2,0,1:T(8,128)(2,1)} %copy.47), channel_id=1, source_target_pairs={{8,0},{16,8},{24,16},{0,24},{9,1},{17,9},{25,17},{1,25},{10,2},{18... | collective-permute-start | bytes 6291464 | tf_op jit(solution)/shard_map/while/body/eval_jaxpr/ppermute | solution.py:23
  1131.6 160.9 %collective-permute-start.1 = (s32[64]{0:T(128)S(1)}, s32[64]{0:T(128)S(1)}, u32[]{:S(2)}, u32[]{:S(2)}) collective-permute-start(s32[64]{0:T(128)S(1)} %copy.46), channel_id=1, source_target_pairs={{1,0},{2,1},{3,2},{4,3},{5,4},{6,5},{7,6},{0,7},{9,8},{10,9},{11,1... | collective-permute-start | bytes 776 | tf_op jit(solution)/shard_map/while/body/eval_jaxpr/ppermute | solution.py:23
  1131.6 160.9 %collective-permute-start.3 = (s32[64]{0:T(128)S(1)}, s32[64]{0:T(128)S(1)}, u32[]{:S(2)}, u32[]{:S(2)}) collective-permute-start(s32[64]{0:T(128)S(1)} %copy.48), channel_id=1, source_target_pairs={{8,0},{16,8},{24,16},{0,24},{9,1},{17,9},{25,17},{1,25},{10,2},{18... | collective-permute-start | bytes 776 | tf_op jit(solution)/shard_map/while/body/eval_jaxpr/ppermute | solution.py:23
  1294.1 164.4 %collective-permute-start = (bf16[64,128,128]{2,0,1:T(8,128)(2,1)S(1)}, bf16[64,128,128]{2,0,1:T(8,128)(2,1)}, u32[]{:S(2)}, u32[]{:S(2)}) collective-permute-start(bf16[64,128,128]{2,0,1:T(8,128)(2,1)S(1)} %copy.45), channel_id=1, source_target_pairs={{1,0},{2,1},{3,2},{4,3},{5,4},{6,5},{7,6},{0,7},{9,8},{10,9},{11,1... | collective-permute-start | bytes 6291464 | tf_op jit(solution)/shard_map/while/body/eval_jaxpr/ppermute | solution.py:23
  1297.3 161.3 %collective-permute-start.2 = (bf16[64,128,128]{2,0,1:T(8,128)(2,1)}, bf16[64,128,128]{2,0,1:T(8,128)(2,1)}, u32[]{:S(2)}, u32[]{:S(2)}) collective-permute-start(bf16[64,128,128]{2,0,1:T(8,128)(2,1)} %copy.47), channel_id=1, source_target_pairs={{8,0},{16,8},{24,16},{0,24},{9,1},{17,9},{25,17},{1,25},{10,2},{18... | collective-permute-start | bytes 6291464 | tf_op jit(solution)/shard_map/while/body/eval_jaxpr/ppermute | solution.py:23
  1298.7 159.9 %collective-permute-start.1 = (s32[64]{0:T(128)S(1)}, s32[64]{0:T(128)S(1)}, u32[]{:S(2)}, u32[]{:S(2)}) collective-permute-start(s32[64]{0:T(128)S(1)} %copy.46), channel_id=1, source_target_pairs={{1,0},{2,1},{3,2},{4,3},{5,4},{6,5},{7,6},{0,7},{9,8},{10,9},{11,1... | collective-permute-start | bytes 776 | tf_op jit(solution)/shard_map/while/body/eval_jaxpr/ppermute | solution.py:23
  1298.7 159.9 %collective-permute-start.3 = (s32[64]{0:T(128)S(1)}, s32[64]{0:T(128)S(1)}, u32[]{:S(2)}, u32[]{:S(2)}) collective-permute-start(s32[64]{0:T(128)S(1)} %copy.48), channel_id=1, source_target_pairs={{8,0},{16,8},{24,16},{0,24},{9,1},{17,9},{25,17},{1,25},{10,2},{18... | collective-permute-start | bytes 776 | tf_op jit(solution)/shard_map/while/body/eval_jaxpr/ppermute | solution.py:23
  1460.2 169.8 %collective-permute-start = (bf16[64,128,128]{2,0,1:T(8,128)(2,1)S(1)}, bf16[64,128,128]{2,0,1:T(8,128)(2,1)}, u32[]{:S(2)}, u32[]{:S(2)}) collective-permute-start(bf16[64,128,128]{2,0,1:T(8,128)(2,1)S(1)} %copy.45), channel_id=1, source_target_pairs={{1,0},{2,1},{3,2},{4,3},{5,4},{6,5},{7,6},{0,7},{9,8},{10,9},{11,1... | collective-permute-start | bytes 6291464 | tf_op jit(solution)/shard_map/while/body/eval_jaxpr/ppermute | solution.py:23
  1467.5 162.5 %collective-permute-start.2 = (bf16[64,128,128]{2,0,1:T(8,128)(2,1)}, bf16[64,128,128]{2,0,1:T(8,128)(2,1)}, u32[]{:S(2)}, u32[]{:S(2)}) collective-permute-start(bf16[64,128,128]{2,0,1:T(8,128)(2,1)} %copy.47), channel_id=1, source_target_pairs={{8,0},{16,8},{24,16},{0,24},{9,1},{17,9},{25,17},{1,25},{10,2},{18... | collective-permute-start | bytes 6291464 | tf_op jit(solution)/shard_map/while/body/eval_jaxpr/ppermute | solution.py:23
  1469.0 160.9 %collective-permute-start.1 = (s32[64]{0:T(128)S(1)}, s32[64]{0:T(128)S(1)}, u32[]{:S(2)}, u32[]{:S(2)}) collective-permute-start(s32[64]{0:T(128)S(1)} %copy.46), channel_id=1, source_target_pairs={{1,0},{2,1},{3,2},{4,3},{5,4},{6,5},{7,6},{0,7},{9,8},{10,9},{11,1... | collective-permute-start | bytes 776 | tf_op jit(solution)/shard_map/while/body/eval_jaxpr/ppermute | solution.py:23
  1469.0 160.9 %collective-permute-start.3 = (s32[64]{0:T(128)S(1)}, s32[64]{0:T(128)S(1)}, u32[]{:S(2)}, u32[]{:S(2)}) collective-permute-start(s32[64]{0:T(128)S(1)} %copy.48), channel_id=1, source_target_pairs={{8,0},{16,8},{24,16},{0,24},{9,1},{17,9},{25,17},{1,25},{10,2},{18... | collective-permute-start | bytes 776 | tf_op jit(solution)/shard_map/while/body/eval_jaxpr/ppermute | solution.py:23
  1631.6 164.4 %collective-permute-start = (bf16[64,128,128]{2,0,1:T(8,128)(2,1)S(1)}, bf16[64,128,128]{2,0,1:T(8,128)(2,1)}, u32[]{:S(2)}, u32[]{:S(2)}) collective-permute-start(bf16[64,128,128]{2,0,1:T(8,128)(2,1)S(1)} %copy.45), channel_id=1, source_target_pairs={{1,0},{2,1},{3,2},{4,3},{5,4},{6,5},{7,6},{0,7},{9,8},{10,9},{11,1... | collective-permute-start | bytes 6291464 | tf_op jit(solution)/shard_map/while/body/eval_jaxpr/ppermute | solution.py:23
  1634.7 161.3 %collective-permute-start.2 = (bf16[64,128,128]{2,0,1:T(8,128)(2,1)}, bf16[64,128,128]{2,0,1:T(8,128)(2,1)}, u32[]{:S(2)}, u32[]{:S(2)}) collective-permute-start(bf16[64,128,128]{2,0,1:T(8,128)(2,1)} %copy.47), channel_id=1, source_target_pairs={{8,0},{16,8},{24,16},{0,24},{9,1},{17,9},{25,17},{1,25},{10,2},{18... | collective-permute-start | bytes 6291464 | tf_op jit(solution)/shard_map/while/body/eval_jaxpr/ppermute | solution.py:23
  1636.1 159.8 %collective-permute-start.1 = (s32[64]{0:T(128)S(1)}, s32[64]{0:T(128)S(1)}, u32[]{:S(2)}, u32[]{:S(2)}) collective-permute-start(s32[64]{0:T(128)S(1)} %copy.46), channel_id=1, source_target_pairs={{1,0},{2,1},{3,2},{4,3},{5,4},{6,5},{7,6},{0,7},{9,8},{10,9},{11,1... | collective-permute-start | bytes 776 | tf_op jit(solution)/shard_map/while/body/eval_jaxpr/ppermute | solution.py:23
  1636.1 159.8 %collective-permute-start.3 = (s32[64]{0:T(128)S(1)}, s32[64]{0:T(128)S(1)}, u32[]{:S(2)}, u32[]{:S(2)}) collective-permute-start(s32[64]{0:T(128)S(1)} %copy.48), channel_id=1, source_target_pairs={{8,0},{16,8},{24,16},{0,24},{9,1},{17,9},{25,17},{1,25},{10,2},{18... | collective-permute-start | bytes 776 | tf_op jit(solution)/shard_map/while/body/eval_jaxpr/ppermute | solution.py:23
  1797.6 165.6 %collective-permute-start = (bf16[64,128,128]{2,0,1:T(8,128)(2,1)S(1)}, bf16[64,128,128]{2,0,1:T(8,128)(2,1)}, u32[]{:S(2)}, u32[]{:S(2)}) collective-permute-start(bf16[64,128,128]{2,0,1:T(8,128)(2,1)S(1)} %copy.45), channel_id=1, source_target_pairs={{1,0},{2,1},{3,2},{4,3},{5,4},{6,5},{7,6},{0,7},{9,8},{10,9},{11,1... | collective-permute-start | bytes 6291464 | tf_op jit(solution)/shard_map/while/body/eval_jaxpr/ppermute | solution.py:23
  1800.7 162.4 %collective-permute-start.2 = (bf16[64,128,128]{2,0,1:T(8,128)(2,1)}, bf16[64,128,128]{2,0,1:T(8,128)(2,1)}, u32[]{:S(2)}, u32[]{:S(2)}) collective-permute-start(bf16[64,128,128]{2,0,1:T(8,128)(2,1)} %copy.47), channel_id=1, source_target_pairs={{8,0},{16,8},{24,16},{0,24},{9,1},{17,9},{25,17},{1,25},{10,2},{18... | collective-permute-start | bytes 6291464 | tf_op jit(solution)/shard_map/while/body/eval_jaxpr/ppermute | solution.py:23
  1802.2 160.9 %collective-permute-start.1 = (s32[64]{0:T(128)S(1)}, s32[64]{0:T(128)S(1)}, u32[]{:S(2)}, u32[]{:S(2)}) collective-permute-start(s32[64]{0:T(128)S(1)} %copy.46), channel_id=1, source_target_pairs={{1,0},{2,1},{3,2},{4,3},{5,4},{6,5},{7,6},{0,7},{9,8},{10,9},{11,1... | collective-permute-start | bytes 776 | tf_op jit(solution)/shard_map/while/body/eval_jaxpr/ppermute | solution.py:23
  1802.2 160.9 %collective-permute-start.3 = (s32[64]{0:T(128)S(1)}, s32[64]{0:T(128)S(1)}, u32[]{:S(2)}, u32[]{:S(2)}) collective-permute-start(s32[64]{0:T(128)S(1)} %copy.48), channel_id=1, source_target_pairs={{8,0},{16,8},{24,16},{0,24},{9,1},{17,9},{25,17},{1,25},{10,2},{18... | collective-permute-start | bytes 776 | tf_op jit(solution)/shard_map/while/body/eval_jaxpr/ppermute | solution.py:23
  2065.8 78.4 %copy-start.1 = (pred[64]{0:T(512)(128)(4,1)S(1)}, pred[64]{0:T(512)(128)(4,1)}, u32[]{:S(2)}) copy-start(pred[64]{0:T(512)(128)(4,1)} %iota_compare_fusion.4) | copy-start | bytes 196
Sparse Core Ops, SparseCore 0:
  21.2 602.5 all-gather.2
